TPU v7x, 32 devices: a whole 2x2x4 slice. The times are simulated.
32 devices in a mesh: ves: 4 (over x, core), shard: 8 (over z, y).
Axes of the slice: x: 2, y: 2, z: 4, core: 2. Of those that a mesh axis runs over, the one named last changes fastest.
Arguments:
- displacement: float32 [3, 8, 256, 128], P(None, 'ves', 'shard'), may hold values from -6 to 6
- tension: float32 [8], P('ves'), may hold values from 2 to 8
- bending: float32 [8], P('ves'), may hold values from 0.2 to 0.8
- offset: float32 [3, 8, 256, 128], P(None, 'ves', 'shard'), may hold values from 0 to 1
- owner: int32 [8, 256, 128], P('ves', 'shard'), may hold values from 0 to 31, as said below
- cell: int32 [8, 256, 128], P('ves', 'shard'), may hold values from 0 to 131071
- populations: float32 [64, 19, 256, 256], P(('ves', 'shard')), may hold values from 0 to 1, as said below
Outputs:
- membrane_force: float32 [3, 8, 256, 128], P(None, 'ves', 'shard')
- force_field: float32 [64, 3, 256, 256], P(('ves', 'shard'))
- new_populations: float32 [64, 19, 256, 256], P(('ves', 'shard'))
Inputs may be any that keep to these rules, and one draw needn't show every extreme that they name: The points of one device name any one owner at most 512 times, and some owner is named exactly 512 times by the points of every device. `populations`: entries are positive.
All inputs are finite; a program needn't handle non-finite values.
Results may differ from a plain program's by a relative error of at most 0.0061.
Values sent between devices are 32-bit elements; how exact they have to be, the bound alone decides.
A program may use at most 128 MiB of HBM per device.

v0:
```python
import math
import jax
import jax.numpy as jnp
from jax import lax
from jax.sharding import PartitionSpec as P

relax_time = 0.8
velocity_x = [0, 1, -1, 0, 0, 0, 1, -1, 0, 0, 0, 1, -1, 0, 0, 1, 1, -1, -1]
velocity_y = [0, 0, 0, 1, -1, 0, 0, 0, 1, -1, 0, 0, 0, 1, -1, 1, -1, 1, -1]
velocity_z = [1, 1, 1, 1, 1, -1, -1, -1, -1, -1, 0, 0, 0, 0, 0, 0, 0, 0, 0]
lattice_weights = [
    1.0 / 18,
    1.0 / 36,
    1.0 / 36,
    1.0 / 36,
    1.0 / 36,
    1.0 / 18,
    1.0 / 36,
    1.0 / 36,
    1.0 / 36,
    1.0 / 36,
    1.0 / 3,
    1.0 / 18,
    1.0 / 18,
    1.0 / 18,
    1.0 / 18,
    1.0 / 36,
    1.0 / 36,
    1.0 / 36,
    1.0 / 36,
]


def padded_2(x, sides, width):
    for axis, dim in sides:
        devices, length = (lax.axis_size(axis), x.shape[dim])
        up = [(i, (i + 1) % devices) for i in range(devices - 1)]
        down = [(j, i) for i, j in up]
        last = lax.slice_in_dim(x, length - width, length, axis=dim)
        initial = lax.slice_in_dim(x, 0, width, axis=dim)
        before = lax.ppermute(last, axis, up)
        after = lax.ppermute(initial, axis, down)
        x = jnp.concatenate([before, x, after], axis=dim)
    return x


def passed_along(value, axis, steps):
    count = lax.axis_size(axis)
    pairs = [(source, (source + steps) % count) for source in range(count)]
    return lax.ppermute(value, axis, pairs)


def kernel_weight(distance):
    return 0.25 * (1.0 + jnp.cos(0.5 * math.pi * distance))


def surface_laplacian(padded):
    center = padded[:, :, 1:-1]
    return (
        padded[:, :, 2:]
        + padded[:, :, :-2]
        + jnp.roll(center, 1, 3)
        + jnp.roll(center, -1, 3)
        - 4.0 * center
    )


def collide(populations, field):
    density = jnp.sum(populations, 1)
    moment_x = jnp.zeros_like(density)
    moment_y = jnp.zeros_like(density)
    moment_z = jnp.zeros_like(density)
    for item in range(19):
        moment_x = moment_x + velocity_x[item] * populations[:, item]
        moment_y = moment_y + velocity_y[item] * populations[:, item]
        moment_z = moment_z + velocity_z[item] * populations[:, item]
    flow_x = (moment_x + 0.5 * field[:, 0]) / density
    flow_y = (moment_y + 0.5 * field[:, 1]) / density
    flow_z = (moment_z + 0.5 * field[:, 2]) / density
    speed_sq = flow_x * flow_x + flow_y * flow_y + flow_z * flow_z
    result = []
    for item in range(19):
        ex, ey, ez = (velocity_x[item], velocity_y[item], velocity_z[item])
        weight = lattice_weights[item]
        along = ex * flow_x + ey * flow_y + ez * flow_z
        equilibrium = weight * density * (1.0 + 3.0 * along + 4.5 * along * along - 1.5 * speed_sq)
        push = (
            (ex - flow_x) * field[:, 0] + (ey - flow_y) * field[:, 1] + (ez - flow_z) * field[:, 2]
        )
        facing = ex * field[:, 0] + ey * field[:, 1] + ez * field[:, 2]
        source = weight * (3.0 * push + 9.0 * along * facing)
        current = populations[:, item]
        result.append(
            current - (current - equilibrium) / relax_time + (1.0 - 0.5 / relax_time) * source
        )
    return jnp.stack(result, 1)


def on_device(displacement, tension, bending, offset, owner, cell, populations):
    padded = padded_2(displacement, (("shard", 2),), 1)
    first = surface_laplacian(padded)
    padded_first = padded_2(first, (("shard", 2),), 1)
    second = surface_laplacian(padded_first)
    membrane_force = tension[None, :, None, None] * first - bending[None, :, None, None] * second
    ves_count = lax.axis_size("ves")
    shard_count = lax.axis_size("shard")
    device_count = ves_count * shard_count
    point_count = owner.size
    capacity = 2 * point_count // device_count
    slot_total = device_count * capacity
    payload = jnp.concatenate(
        [membrane_force.reshape(3, point_count), offset.reshape(3, point_count)], 0
    )
    owner_flat = owner.reshape(point_count)
    cell_flat = cell.reshape(point_count)
    order = jnp.argsort(owner_flat, stable=True)
    sorted_owner = owner_flat[order]
    matches = sorted_owner[:, None] == jnp.arange(device_count, dtype=jnp.int32)[None, :]
    counts = jnp.sum(matches.astype(jnp.int32), 0)
    starts = jnp.cumsum(counts) - counts
    first_place = jnp.sum(jnp.where(matches, starts[None, :], 0), 1)
    slot = sorted_owner * capacity + jnp.arange(point_count, dtype=jnp.int32) - first_place
    send_values = jnp.zeros((6, slot_total), jnp.float32).at[:, slot].set(payload[:, order])
    send_cells = jnp.zeros((1, slot_total), jnp.int32).at[0, slot].set(cell_flat[order])
    got_values, got_cells = (
        lax.all_to_all(
            send_values.reshape(6, device_count, capacity),
            ("ves", "shard"),
            split_axis=1,
            concat_axis=1,
            tiled=True,
        ),
        lax.all_to_all(
            send_cells.reshape(1, device_count, capacity),
            ("ves", "shard"),
            split_axis=1,
            concat_axis=1,
            tiled=True,
        ),
    )
    got_values = got_values.reshape(6, slot_total)
    got_cells = got_cells.reshape(slot_total)
    slab = populations.shape[0]
    width = populations.shape[2]
    depth = slab + 3
    block = min(1024, slot_total)
    turns = slot_total // block
    value_blocks = got_values.reshape(6, turns, block).transpose(1, 0, 2)
    cell_blocks = got_cells.reshape(turns, block)
    grid = jnp.arange(width, dtype=jnp.int32)
    layers = jnp.arange(depth, dtype=jnp.int32)

    def spread_block(total, items):
        values, cells = items
        plane = cells // (width * width)
        column_x = cells // width % width
        column_y = cells % width
        weight_x = jnp.zeros((block, width), jnp.float32)
        weight_y = jnp.zeros((block, width), jnp.float32)
        weight_z = jnp.zeros((block, depth), jnp.float32)
        for reach in range(-1, 3):
            weight_x = weight_x + jnp.where(
                grid[None, :] == ((column_x + reach) % width)[:, None],
                kernel_weight(values[3] - reach)[:, None],
                0.0,
            )
            weight_y = weight_y + jnp.where(
                grid[None, :] == ((column_y + reach) % width)[:, None],
                kernel_weight(values[4] - reach)[:, None],
                0.0,
            )
            weight_z = weight_z + jnp.where(
                layers[None, :] == (plane + reach + 1)[:, None],
                kernel_weight(values[5] - reach)[:, None],
                0.0,
            )
        scaled = values[0:3].T[:, None, :, None] * weight_z[:, :, None, None]
        left = (
            (scaled * weight_x[:, None, None, :])
            .astype(jnp.bfloat16)
            .reshape(block, depth * 3 * width)
        )
        right = weight_y.astype(jnp.bfloat16)
        product = lax.dot_general(
            left, right, (((0,), (0,)), ((), ())), preferred_element_type=jnp.float32
        )
        return (total + product, None)

    total, unused = lax.scan(
        spread_block,
        jnp.zeros((depth * 3 * width, width), jnp.float32),
        (value_blocks, cell_blocks),
    )
    spread = total.reshape(depth, 3, width, width)
    from_below = passed_along(spread[slab + 1 : slab + 3], ("ves", "shard"), 1)
    from_above = passed_along(spread[0:1], ("ves", "shard"), -1)
    force_field = spread[1 : slab + 1].at[0:2].add(from_below).at[slab - 1 : slab].add(from_above)
    post = collide(populations, force_field)
    low_part = passed_along(post[slab - 1, 0:5], ("ves", "shard"), 1)
    high_part = passed_along(post[0, 5:10], ("ves", "shard"), -1)
    low_source = jnp.concatenate([low_part[None], post[: slab - 1, 0:5]], 0)
    high_source = jnp.concatenate([post[1:, 5:10], high_part[None]], 0)
    source = jnp.concatenate([low_source, high_source, post[:, 10:]], 1)
    moved = [
        jnp.roll(source[:, item], (velocity_x[item], velocity_y[item]), (1, 2))
        for item in range(19)
    ]
    return (membrane_force, force_field, jnp.stack(moved, 1))


def solution(mesh):
    return jax.shard_map(
        on_device,
        mesh=mesh,
        in_specs=(
            P(None, "ves", "shard", None),
            P("ves"),
            P("ves"),
            P(None, "ves", "shard", None),
            P("ves", "shard", None),
            P("ves", "shard", None),
            P(("ves", "shard"), None, None, None),
        ),
        out_specs=(
            P(None, "ves", "shard", None),
            P(("ves", "shard"), None, None, None),
            P(("ves", "shard"), None, None, None),
        ),
        check_vma=False,
    )
```

profile of v0, /device:TPU:0, one launch (start us, length us, event | category | flops | bytes accessed | tf_op | source)
XLA Modules:
  0.0 650.7 jit_solution(11068581569204606611)
XLA Ops:
  1.4 4.9 collective-permute-start.1
  7.6 7.5 %sort.17 = (s32[8192]{0:T(1024)}, s32[8192]{0:T(1024)S(1)}) sort(s32[8192]{0:T(1024)} %bitcast.1380, s32[8192]{0:T(1024)S(1)} %iota.38), dimensions={0}, to_apply=%region_0.1 | sort | flops 106496 | bytes 131072 | tf_op jit(solution)/shard_map/jit(argsort)/sort | solution.py:116
  15.2 45.5 %gather_fusion = s32[8192]{0:T(1024)S(1)} fusion(s32[8192]{0:T(1024)S(1)} %bitcast.1381, s32[8192]{0:T(1024)S(1)} %fusion.372), kind=kCustom, calls=%fused_computation | custom fusion | bytes 98304 | tf_op jit(solution)/shard_map/gather | solution.py:117
  62.0 45.5 %gather_fusion.1 = s32[8192]{0:T(1024)S(1)} fusion(s32[8192]{0:T(1024)S(1)} %bitcast.1379, s32[8192]{0:T(1024)S(1)} %fusion.372), kind=kCustom, calls=%fused_computation.2 | custom fusion | bytes 98304 | tf_op jit(solution)/shard_map/gather | solution.py:124
  107.5 31.1 %scatter_custom_fusion.1 = s32[16384]{0:T(1024)} fusion(s32[8192]{0:T(1024)S(1)} %broadcast_select_fusion, s32[8192]{0:T(1024)S(1)} %gather_fusion.1, s32[]{:T(128)} %constant.337.clone.1), kind=kCustom, calls=%fused_computation.665 | custom fusion | bytes 65540
  138.6 7.0 %all-to-all-start.1 = ((s32[1,32,512]{2,0,1:T(1,128)}), s32[1,32,512]{2,0,1:T(1,128)S(1)}, u32[]{:S(2)}, u32[]{:S(2)}) async-start(s32[1,32,512]{2,0,1:T(1,128)} %bitcast.8), calls=%async_computation.1 | async-start | bytes 131072 | tf_op jit(solution)/shard_map/all_to_all | solution.py:133
  146.0 3.7 collective-permute-start.3
  151.1 4.1 collective-permute-done.2
  155.6 2.7 copy.148
  158.2 70.3 %scatter_custom_fusion = f32[6,16384]{0,1:T(8,128)} fusion(s32[8192]{0:T(1024)S(1)} %bitcast.1413, f32[6,8192]{0,1:T(8,128)} %copy.148, s32[8192]{0:T(1024)S(1)} %fusion.372, f32[]{:T(128)} %constant.338.clone.1), kind=kCustom, calls=%fused_computation.104 | custom fusion | bytes 393728 | tf_op jit(solution)/shard_map/scatter | solution.py:123
  228.5 6.0 copy.149
  234.5 6.0 all-to-all-start
  240.8 16.0 %all-to-all-done = f32[6,32,512]{2,0,1:T(8,128)S(1)} async-done(((f32[6,32,512]{2,0,1:T(8,128)}), f32[6,32,512]{2,0,1:T(8,128)S(1)}, u32[]{:S(2)}, u32[]{:S(2)}) %all-to-all-start) | async-done | bytes 393248 | tf_op jit(solution)/shard_map/all_to_all | solution.py:126
  257.2 253.5 %while.18 = (s32[]{:T(128)}, f32[3840,256]{1,0:T(8,128)}, f32[16,6,1024]{2,0,1:T(8,128)S(1)}, s32[16,1024]{1,0:T(8,128)S(1)}, s32[]{:T(128)}, /*index=5*/s32[]{:T(128)}, s32[]{}, s32[]{}, s32[]{}) while((s32[]{:T(128)}, f32[3840,256]{1,0:T(8,128)}, f32[16,6,1024]{2,0,1:T(8,128)S(1)}, s32[16,1024]{1,0:T(8,128)S(1)}, ...), condition=%wide.region_7.8_spmd.clone.clone, body=%wide.region_6.7_spmd.clone.clone.sunk | while | flops 2029383680 | bytes 26144940 | solution.py:189
  257.2 1.3 add_multiply_fusion.15
  259.1 5.4 multiply_convert_fusion.2
  264.5 7.5 %convolution_add_fusion.2 = f32[3840,256]{1,0:T(8,128)} fusion(bf16[1024,3840]{0,1:T(8,128)(2,1)} %bitcast.1382, f32[3840,256]{1,0:T(8,128)} %get-tuple-element.434, pred[]{:T(512)S(6)} %compare.117, f32[1024]{0:T(1024)S(1)} %bitcast.1419, s32[1024]{0:T(1024)S(1)} %get-tuple-element.417, f32[1024]{0:T(1024)S(1)} %bitcast.1418, ...), kind=kOutput, calls=%fused_computation.8.clone.1 | convolution fusion | flops 2018377728 | bytes 15761409 | tf_op jit(solution)/shard_map/while/body/eval_jaxpr/dot_general | solution.py:184
  272.0 1.3 add_multiply_fusion.15
  273.8 5.4 multiply_convert_fusion.2
  279.3 8.6 %convolution_add_fusion.2 = f32[3840,256]{1,0:T(8,128)} fusion(bf16[1024,3840]{0,1:T(8,128)(2,1)} %bitcast.1382, f32[3840,256]{1,0:T(8,128)} %get-tuple-element.434, pred[]{:T(512)S(6)} %compare.117, f32[1024]{0:T(1024)S(1)} %bitcast.1419, s32[1024]{0:T(1024)S(1)} %get-tuple-element.417, f32[1024]{0:T(1024)S(1)} %bitcast.1418, ...), kind=kOutput, calls=%fused_computation.8.clone.1 | convolution fusion | flops 2018377728 | bytes 15761409 | tf_op jit(solution)/shard_map/while/body/eval_jaxpr/dot_general | solution.py:184
  287.9 1.3 add_multiply_fusion.15
  289.8 5.4 multiply_convert_fusion.2
  295.2 8.6 %convolution_add_fusion.2 = f32[3840,256]{1,0:T(8,128)} fusion(bf16[1024,3840]{0,1:T(8,128)(2,1)} %bitcast.1382, f32[3840,256]{1,0:T(8,128)} %get-tuple-element.434, pred[]{:T(512)S(6)} %compare.117, f32[1024]{0:T(1024)S(1)} %bitcast.1419, s32[1024]{0:T(1024)S(1)} %get-tuple-element.417, f32[1024]{0:T(1024)S(1)} %bitcast.1418, ...), kind=kOutput, calls=%fused_computation.8.clone.1 | convolution fusion | flops 2018377728 | bytes 15761409 | tf_op jit(solution)/shard_map/while/body/eval_jaxpr/dot_general | solution.py:184
  303.8 1.3 add_multiply_fusion.15
  305.7 5.4 multiply_convert_fusion.2
  311.1 8.6 %convolution_add_fusion.2 = f32[3840,256]{1,0:T(8,128)} fusion(bf16[1024,3840]{0,1:T(8,128)(2,1)} %bitcast.1382, f32[3840,256]{1,0:T(8,128)} %get-tuple-element.434, pred[]{:T(512)S(6)} %compare.117, f32[1024]{0:T(1024)S(1)} %bitcast.1419, s32[1024]{0:T(1024)S(1)} %get-tuple-element.417, f32[1024]{0:T(1024)S(1)} %bitcast.1418, ...), kind=kOutput, calls=%fused_computation.8.clone.1 | convolution fusion | flops 2018377728 | bytes 15761409 | tf_op jit(solution)/shard_map/while/body/eval_jaxpr/dot_general | solution.py:184
  319.7 1.3 add_multiply_fusion.15
  321.6 5.4 multiply_convert_fusion.2
  327.0 8.6 %convolution_add_fusion.2 = f32[3840,256]{1,0:T(8,128)} fusion(bf16[1024,3840]{0,1:T(8,128)(2,1)} %bitcast.1382, f32[3840,256]{1,0:T(8,128)} %get-tuple-element.434, pred[]{:T(512)S(6)} %compare.117, f32[1024]{0:T(1024)S(1)} %bitcast.1419, s32[1024]{0:T(1024)S(1)} %get-tuple-element.417, f32[1024]{0:T(1024)S(1)} %bitcast.1418, ...), kind=kOutput, calls=%fused_computation.8.clone.1 | convolution fusion | flops 2018377728 | bytes 15761409 | tf_op jit(solution)/shard_map/while/body/eval_jaxpr/dot_general | solution.py:184
  337.5 5.4 multiply_convert_fusion.2
  342.9 8.6 %convolution_add_fusion.2 = f32[3840,256]{1,0:T(8,128)} fusion(bf16[1024,3840]{0,1:T(8,128)(2,1)} %bitcast.1382, f32[3840,256]{1,0:T(8,128)} %get-tuple-element.434, pred[]{:T(512)S(6)} %compare.117, f32[1024]{0:T(1024)S(1)} %bitcast.1419, s32[1024]{0:T(1024)S(1)} %get-tuple-element.417, f32[1024]{0:T(1024)S(1)} %bitcast.1418, ...), kind=kOutput, calls=%fused_computation.8.clone.1 | convolution fusion | flops 2018377728 | bytes 15761409 | tf_op jit(solution)/shard_map/while/body/eval_jaxpr/dot_general | solution.py:184
  353.4 5.4 multiply_convert_fusion.2
  358.8 8.6 %convolution_add_fusion.2 = f32[3840,256]{1,0:T(8,128)} fusion(bf16[1024,3840]{0,1:T(8,128)(2,1)} %bitcast.1382, f32[3840,256]{1,0:T(8,128)} %get-tuple-element.434, pred[]{:T(512)S(6)} %compare.117, f32[1024]{0:T(1024)S(1)} %bitcast.1419, s32[1024]{0:T(1024)S(1)} %get-tuple-element.417, f32[1024]{0:T(1024)S(1)} %bitcast.1418, ...), kind=kOutput, calls=%fused_computation.8.clone.1 | convolution fusion | flops 2018377728 | bytes 15761409 | tf_op jit(solution)/shard_map/while/body/eval_jaxpr/dot_general | solution.py:184
  369.3 5.4 multiply_convert_fusion.2
  374.7 8.6 %convolution_add_fusion.2 = f32[3840,256]{1,0:T(8,128)} fusion(bf16[1024,3840]{0,1:T(8,128)(2,1)} %bitcast.1382, f32[3840,256]{1,0:T(8,128)} %get-tuple-element.434, pred[]{:T(512)S(6)} %compare.117, f32[1024]{0:T(1024)S(1)} %bitcast.1419, s32[1024]{0:T(1024)S(1)} %get-tuple-element.417, f32[1024]{0:T(1024)S(1)} %bitcast.1418, ...), kind=kOutput, calls=%fused_computation.8.clone.1 | convolution fusion | flops 2018377728 | bytes 15761409 | tf_op jit(solution)/shard_map/while/body/eval_jaxpr/dot_general | solution.py:184
  385.2 5.4 multiply_convert_fusion.2
  390.6 8.6 %convolution_add_fusion.2 = f32[3840,256]{1,0:T(8,128)} fusion(bf16[1024,3840]{0,1:T(8,128)(2,1)} %bitcast.1382, f32[3840,256]{1,0:T(8,128)} %get-tuple-element.434, pred[]{:T(512)S(6)} %compare.117, f32[1024]{0:T(1024)S(1)} %bitcast.1419, s32[1024]{0:T(1024)S(1)} %get-tuple-element.417, f32[1024]{0:T(1024)S(1)} %bitcast.1418, ...), kind=kOutput, calls=%fused_computation.8.clone.1 | convolution fusion | flops 2018377728 | bytes 15761409 | tf_op jit(solution)/shard_map/while/body/eval_jaxpr/dot_general | solution.py:184
  401.2 5.4 multiply_convert_fusion.2
  406.6 8.6 %convolution_add_fusion.2 = f32[3840,256]{1,0:T(8,128)} fusion(bf16[1024,3840]{0,1:T(8,128)(2,1)} %bitcast.1382, f32[3840,256]{1,0:T(8,128)} %get-tuple-element.434, pred[]{:T(512)S(6)} %compare.117, f32[1024]{0:T(1024)S(1)} %bitcast.1419, s32[1024]{0:T(1024)S(1)} %get-tuple-element.417, f32[1024]{0:T(1024)S(1)} %bitcast.1418, ...), kind=kOutput, calls=%fused_computation.8.clone.1 | convolution fusion | flops 2018377728 | bytes 15761409 | tf_op jit(solution)/shard_map/while/body/eval_jaxpr/dot_general | solution.py:184
  417.1 5.4 multiply_convert_fusion.2
  422.5 8.6 %convolution_add_fusion.2 = f32[3840,256]{1,0:T(8,128)} fusion(bf16[1024,3840]{0,1:T(8,128)(2,1)} %bitcast.1382, f32[3840,256]{1,0:T(8,128)} %get-tuple-element.434, pred[]{:T(512)S(6)} %compare.117, f32[1024]{0:T(1024)S(1)} %bitcast.1419, s32[1024]{0:T(1024)S(1)} %get-tuple-element.417, f32[1024]{0:T(1024)S(1)} %bitcast.1418, ...), kind=kOutput, calls=%fused_computation.8.clone.1 | convolution fusion | flops 2018377728 | bytes 15761409 | tf_op jit(solution)/shard_map/while/body/eval_jaxpr/dot_general | solution.py:184
  433.0 5.4 multiply_convert_fusion.2
  438.4 8.6 %convolution_add_fusion.2 = f32[3840,256]{1,0:T(8,128)} fusion(bf16[1024,3840]{0,1:T(8,128)(2,1)} %bitcast.1382, f32[3840,256]{1,0:T(8,128)} %get-tuple-element.434, pred[]{:T(512)S(6)} %compare.117, f32[1024]{0:T(1024)S(1)} %bitcast.1419, s32[1024]{0:T(1024)S(1)} %get-tuple-element.417, f32[1024]{0:T(1024)S(1)} %bitcast.1418, ...), kind=kOutput, calls=%fused_computation.8.clone.1 | convolution fusion | flops 2018377728 | bytes 15761409 | tf_op jit(solution)/shard_map/while/body/eval_jaxpr/dot_general | solution.py:184
  448.9 5.4 multiply_convert_fusion.2
  454.3 8.6 %convolution_add_fusion.2 = f32[3840,256]{1,0:T(8,128)} fusion(bf16[1024,3840]{0,1:T(8,128)(2,1)} %bitcast.1382, f32[3840,256]{1,0:T(8,128)} %get-tuple-element.434, pred[]{:T(512)S(6)} %compare.117, f32[1024]{0:T(1024)S(1)} %bitcast.1419, s32[1024]{0:T(1024)S(1)} %get-tuple-element.417, f32[1024]{0:T(1024)S(1)} %bitcast.1418, ...), kind=kOutput, calls=%fused_computation.8.clone.1 | convolution fusion | flops 2018377728 | bytes 15761409 | tf_op jit(solution)/shard_map/while/body/eval_jaxpr/dot_general | solution.py:184
  464.8 5.4 multiply_convert_fusion.2
  470.2 8.6 %convolution_add_fusion.2 = f32[3840,256]{1,0:T(8,128)} fusion(bf16[1024,3840]{0,1:T(8,128)(2,1)} %bitcast.1382, f32[3840,256]{1,0:T(8,128)} %get-tuple-element.434, pred[]{:T(512)S(6)} %compare.117, f32[1024]{0:T(1024)S(1)} %bitcast.1419, s32[1024]{0:T(1024)S(1)} %get-tuple-element.417, f32[1024]{0:T(1024)S(1)} %bitcast.1418, ...), kind=kOutput, calls=%fused_computation.8.clone.1 | convolution fusion | flops 2018377728 | bytes 15761409 | tf_op jit(solution)/shard_map/while/body/eval_jaxpr/dot_general | solution.py:184
  480.7 5.4 multiply_convert_fusion.2
  486.1 8.6 %convolution_add_fusion.2 = f32[3840,256]{1,0:T(8,128)} fusion(bf16[1024,3840]{0,1:T(8,128)(2,1)} %bitcast.1382, f32[3840,256]{1,0:T(8,128)} %get-tuple-element.434, pred[]{:T(512)S(6)} %compare.117, f32[1024]{0:T(1024)S(1)} %bitcast.1419, s32[1024]{0:T(1024)S(1)} %get-tuple-element.417, f32[1024]{0:T(1024)S(1)} %bitcast.1418, ...), kind=kOutput, calls=%fused_computation.8.clone.1 | convolution fusion | flops 2018377728 | bytes 15761409 | tf_op jit(solution)/shard_map/while/body/eval_jaxpr/dot_general | solution.py:184
  496.6 5.4 multiply_convert_fusion.2
  502.0 8.6 %convolution_add_fusion.2 = f32[3840,256]{1,0:T(8,128)} fusion(bf16[1024,3840]{0,1:T(8,128)(2,1)} %bitcast.1382, f32[3840,256]{1,0:T(8,128)} %get-tuple-element.434, pred[]{:T(512)S(6)} %compare.117, f32[1024]{0:T(1024)S(1)} %bitcast.1419, s32[1024]{0:T(1024)S(1)} %get-tuple-element.417, f32[1024]{0:T(1024)S(1)} %bitcast.1418, ...), kind=kOutput, calls=%fused_computation.8.clone.1 | convolution fusion | flops 2018377728 | bytes 15761409 | tf_op jit(solution)/shard_map/while/body/eval_jaxpr/dot_general | solution.py:184
  510.7 3.7 fusion.382
  516.5 4.6 collective-permute-start.5
  521.2 4.7 reduce_sum.34
  525.9 40.6 %collective-permute-done.4 = f32[2,3,256,256]{3,2,1,0:T(8,128)} collective-permute-done((f32[2,3,256,256]{3,2,1,0:T(8,128)}, f32[2,3,256,256]{3,2,1,0:T(8,128)}, u32[]{:S(2)}, u32[]{:S(2)}) %collective-permute-start.4) | collective-permute-done | bytes 1572896 | tf_op jit(solution)/shard_map/ppermute | solution.py:50
  566.5 2.2 add.2902
  569.9 1.3 fusion.29
  571.2 5.9 fusion.77
  577.2 2.4 fusion.174
  585.8 1.4 collective-permute-start.6
  587.2 1.7 fusion.160
  588.8 1.6 fusion.167
  592.4 50.1 %collective-permute-done.6 = f32[5,256,256]{2,1,0:T(8,128)S(1)} collective-permute-done((f32[5,256,256]{2,1,0:T(8,128)S(1)}, f32[5,256,256]{2,1,0:T(8,128)S(1)}, u32[]{:S(2)}, u32[]{:S(2)}) %collective-permute-start.6) | collective-permute-done | bytes 1310752 | tf_op jit(solution)/shard_map/ppermute | solution.py:50
  646.6 3.9 copy-done.7
  (264 shorter events, 43.5 us)
Async XLA Ops:
  0.6 61.3 %copy-start = (s32[2,32,128]{2,1,0:T(8,128)S(1)}, s32[2,32,128]{2,1,0:T(8,128)}, u32[]{:S(2)}) copy-start(s32[2,32,128]{2,1,0:T(8,128)} %param.20) | copy-start | bytes 98308
  0.6 14.5 %copy-start.2 = (s32[2,32,128]{2,1,0:T(8,128)S(1)}, s32[2,32,128]{2,1,0:T(8,128)}, u32[]{:S(2)}) copy-start(s32[2,32,128]{2,1,0:T(8,128)} %param.19) | copy-start | bytes 98308
  1.4 144.4 %collective-permute-start.1 = (f32[3,2,1,128]{3,2,1,0:T(1,128)S(1)}, f32[3,2,1,128]{3,2,1,0:T(1,128)S(1)}, u32[]{:S(2)}, u32[]{:S(2)}) collective-permute-start(f32[3,2,1,128]{3,2,1,0:T(1,128)S(1)} %get-tuple-element.346), channel_id=1, source_target_pairs={{0,1},{1,2},{2,3},{3,4},{4,5},{5,6},{6,7},{8,9},{9,10},{10,11},{11... | collective-permute-start | bytes 9224 | tf_op jit(solution)/shard_map/ppermute | solution.py:41
  6.3 139.5 %collective-permute-start = (f32[3,2,1,128]{3,2,1,0:T(1,128)S(1)}, f32[3,2,1,128]{3,2,1,0:T(1,128)S(1)}, u32[]{:S(2)}, u32[]{:S(2)}) collective-permute-start(f32[3,2,1,128]{3,2,1,0:T(1,128)S(1)} %get-tuple-element.345), channel_id=1, source_target_pairs={{1,0},{2,1},{3,2},{4,3},{5,4},{6,5},{7,6},{9,8},{10,9},{11,10},{12... | collective-permute-start | bytes 9224 | tf_op jit(solution)/shard_map/ppermute | solution.py:42
  15.2 46.4 %copy-start.11 = (s32[2]{0:T(128)S(1)}, s32[2]{0:T(128)}, u32[]{:S(2)}) copy-start(s32[2]{0:T(128)} %constant.369) | copy-start | bytes 28
  15.2 46.6 %copy-start.10 = (s32[2]{0:T(128)S(1)}, s32[2]{0:T(128)}, u32[]{:S(2)}) copy-start(s32[2]{0:T(128)} %constant.366) | copy-start | bytes 28
  61.9 83.6 %copy-start.4 = (f32[3,2,32,128]{3,2,1,0:T(8,128)S(1)}, f32[3,2,32,128]{3,2,1,0:T(8,128)}, u32[]{:S(2)}) copy-start(f32[3,2,32,128]{3,2,1,0:T(8,128)} %param.15) | copy-start | bytes 294916
  62.0 93.2 %copy-start.8 = (f32[2]{0:T(128)S(1)}, f32[2]{0:T(128)}, u32[]{:S(2)}) copy-start(f32[2]{0:T(128)} %param.17) | copy-start | bytes 28
  62.0 93.2 %copy-start.9 = (f32[2]{0:T(128)S(1)}, f32[2]{0:T(128)}, u32[]{:S(2)}) copy-start(f32[2]{0:T(128)} %param.16) | copy-start | bytes 28
  62.0 93.4 %copy-start.6 = (f32[3,2,32,128]{3,2,1,0:T(8,128)S(1)}, f32[3,2,32,128]{3,2,1,0:T(8,128)}, u32[]{:S(2)}) copy-start(f32[3,2,32,128]{3,2,1,0:T(8,128)} %param.18) | copy-start | bytes 294916
  138.6 95.9 %all-to-all-start.1 = ((s32[1,32,512]{2,0,1:T(1,128)}), s32[1,32,512]{2,0,1:T(1,128)S(1)}, u32[]{:S(2)}, u32[]{:S(2)}) async-start(s32[1,32,512]{2,0,1:T(1,128)} %bitcast.8), calls=%async_computation.1 | async-start | bytes 131072 | tf_op jit(solution)/shard_map/all_to_all | solution.py:133
  146.0 5.1 collective-permute-start.3
  149.7 5.5 collective-permute-start.2
  155.3 73.2 %copy-start.5 = (f32[3,2,32,128]{3,2,1,0:T(8,128)}, f32[3,2,32,128]{3,2,1,0:T(8,128)S(1)}, u32[]{:S(2)}) copy-start(f32[3,2,32,128]{3,2,1,0:T(8,128)S(1)} %fusion.366) | copy-start | bytes 294916
  234.5 22.3 %all-to-all-start = ((f32[6,32,512]{2,0,1:T(8,128)}), f32[6,32,512]{2,0,1:T(8,128)S(1)}, u32[]{:S(2)}, u32[]{:S(2)}) async-start(f32[6,32,512]{2,0,1:T(8,128)} %copy.149), calls=%async_computation | async-start | bytes 1048576 | tf_op jit(solution)/shard_map/all_to_all | solution.py:126
  514.4 52.0 %collective-permute-start.4 = (f32[2,3,256,256]{3,2,1,0:T(8,128)}, f32[2,3,256,256]{3,2,1,0:T(8,128)}, u32[]{:S(2)}, u32[]{:S(2)}) collective-permute-start(f32[2,3,256,256]{3,2,1,0:T(8,128)} %bitcast.10), channel_id=1, source_target_pairs={{0,1},{1,2},{2,3},{3,4},{4,5},{5,6},{6,7},{7,8},{8,9},{9,10},{10,1... | collective-permute-start | bytes 4718600 | tf_op jit(solution)/shard_map/ppermute | solution.py:50
  516.5 53.3 %collective-permute-start.5 = (f32[1,3,256,256]{3,2,1,0:T(8,128)S(1)}, f32[1,3,256,256]{3,2,1,0:T(8,128)}, u32[]{:S(2)}, u32[]{:S(2)}) collective-permute-start(f32[1,3,256,256]{3,2,1,0:T(8,128)S(1)} %bitcast.1401), channel_id=1, source_target_pairs={{0,31},{1,0},{2,1},{3,2},{4,3},{5,4},{6,5},{7,6},{8,7},{9,8},{10,9... | collective-permute-start | bytes 2359304 | tf_op jit(solution)/shard_map/ppermute | solution.py:50
  521.2 56.0 %slice-start = ((s8[9961472]{0:T(1024)(128)(4,1)}), s8[1572864]{0:T(1024)(128)(4,1)S(1)}, s32[]{:S(2)}) async-start(s8[9961472]{0:T(1024)(128)(4,1)} %bitcast.1383), calls=%async_computation.2 | async-start | bytes 3145728
  566.5 10.7 %slice-start.1 = ((s8[9961472]{0:T(1024)(128)(4,1)}), s8[4194304]{0:T(1024)(128)(4,1)S(1)}, s32[]{:S(2)}) async-start(s8[9961472]{0:T(1024)(128)(4,1)} %bitcast.1383), calls=%async_computation.3 | async-start | bytes 8388608
  571.2 73.5 %copy-start.3 = (f32[2,3,256,256]{3,2,1,0:T(8,128)}, f32[2,3,256,256]{3,2,1,0:T(8,128)S(1)}, u32[]{:S(2)}) copy-start(f32[2,3,256,256]{3,2,1,0:T(8,128)S(1)} %fusion.29) | copy-start | bytes 4718596
  571.2 6.0 slice-start.2
  584.6 59.0 %collective-permute-start.7 = (f32[5,256,256]{2,1,0:T(8,128)S(1)}, f32[5,256,256]{2,1,0:T(8,128)S(1)}, u32[]{:S(2)}, u32[]{:S(2)}) collective-permute-start(f32[5,256,256]{2,1,0:T(8,128)S(1)} %get-tuple-element.327), channel_id=1, source_target_pairs={{0,31},{1,0},{2,1},{3,2},{4,3},{5,4},{6,5},{7,6},{8,7},{9,8},{10,9... | collective-permute-start | bytes 3932168 | tf_op jit(solution)/shard_map/ppermute | solution.py:50
  585.8 56.7 %collective-permute-start.6 = (f32[5,256,256]{2,1,0:T(8,128)S(1)}, f32[5,256,256]{2,1,0:T(8,128)S(1)}, u32[]{:S(2)}, u32[]{:S(2)}) collective-permute-start(f32[5,256,256]{2,1,0:T(8,128)S(1)} %get-tuple-element.334), channel_id=1, source_target_pairs={{0,1},{1,2},{2,3},{3,4},{4,5},{5,6},{6,7},{7,8},{8,9},{9,10},{10,1... | collective-permute-start | bytes 3932168 | tf_op jit(solution)/shard_map/ppermute | solution.py:50
  645.5 5.0 copy-start.1
  646.5 3.9 copy-start.7
where the time goes:
time: 660 us; the launch traced here: 651 us
  local copies, waits for them, and re-layouts  214 us (32%)
  other arithmetic  153 us (23%)
  matrix products  137 us (21%)
  waiting for transfers between devices  112 us (17%)
  starting transfers between devices  32.1 us (5%)
    dot_general x16, matrix products, spread_block(): lax.dot_general(left, right, (((0,), (0,)), ((), ())), preferred_element_...  137 us
    ppermute x4, waiting for transfers between devices, passed_along(): return lax.ppermute(value, axis, pairs)  91.9 us
    convert_element_type x16, other arithmetic, spread_block(): left = (scaled * weight_x[:, None, None, :]).astype(jnp.bfloat16).reshape...  86.4 us
    scatter x1, local copies, waits for them, and re-layouts, on_device(): jnp.zeros((6, slot_total), jnp.float32).at[:, slot].set(payload[:, order])  70.3 us
    gather x1, local copies, waits for them, and re-layouts, on_device(): cell_flat[order]  45.5 us
    gather x1, local copies, waits for them, and re-layouts, on_device(): sorted_owner = owner_flat[order]  45.5 us
    unnamed x31, local copies, waits for them, and re-layouts  35.1 us
    mul x16, other arithmetic, kernel_weight(): return 0.25 * (1.0 + jnp.cos(0.5 * math.pi * distance))  20.8 us
  transfers between devices with their start and end apart: 10, of which 5 were waited for; matrix products, arithmetic and copies ran while one was open for 35% of the time, Pallas kernels for 0%

commit v1 on v0

--- a/solution.py
+++ b/solution.py
@@ -123,12 +123,20 @@
     send_values = jnp.zeros((6, slot_total), jnp.float32).at[:, slot].set(payload[:, order])
     send_cells = jnp.zeros((1, slot_total), jnp.int32).at[0, slot].set(cell_flat[order])
     got_values, got_cells = (
-        lax.all_to_all(
-            send_values.reshape(6, device_count, capacity),
-            ("ves", "shard"),
-            split_axis=1,
-            concat_axis=1,
-            tiled=True,
+        jnp.concatenate(
+            lax.all_to_all(
+                jnp.stack(
+                    jnp.split(
+                        send_values.reshape(6, device_count, capacity),
+                        lax.axis_size(("ves", "shard")),
+                        axis=1,
+                    )
+                ),
+                ("ves", "shard"),
+                0,
+                0,
+            ),
+            axis=1,
         ),
         lax.all_to_all(
             send_cells.reshape(1, device_count, capacity),

time: 660 us -> 713 us (1.080)
  local copies, waits for them, and re-layouts: 214 us -> 270 us
    unnamed x31 -> x94, local copies, waits for them, and re-layouts: 35.1 us -> 88.5 us
    split x0 -> x2, local copies, waits for them, and re-layouts: none -> 7.38 us  [on_device(): jnp.split(send_values.reshape(6, device_count, capacity), lax.axis_size((...]
  transfers between devices with their start and end apart: 10 -> 10, of which waited for: 5 -> 5; matrix products, arithmetic and copies ran while one was open for 35% -> 40% of each run, Pallas kernels for 0% -> 0%
where the time goes in v1:
time: 713 us; the launch traced here: 703 us
  local copies, waits for them, and re-layouts  270 us (38%)
  other arithmetic  154 us (22%)
  matrix products  137 us (19%)
  waiting for transfers between devices  108 us (15%)
  starting transfers between devices  31.6 us (4%)
    dot_general x16, matrix products, spread_block(): lax.dot_general(left, right, (((0,), (0,)), ((), ())), preferred_element_...  137 us
    ppermute x4, waiting for transfers between devices, passed_along(): return lax.ppermute(value, axis, pairs)  91.9 us
    unnamed x94, local copies, waits for them, and re-layouts  88.5 us
    convert_element_type x16, other arithmetic, spread_block(): left = (scaled * weight_x[:, None, None, :]).astype(jnp.bfloat16).reshape...  86.4 us
    scatter x1, local copies, waits for them, and re-layouts, on_device(): jnp.zeros((6, slot_total), jnp.float32).at[:, slot].set(payload[:, order])  70.9 us
    gather x1, local copies, waits for them, and re-layouts, on_device(): cell_flat[order]  45.5 us
    gather x1, local copies, waits for them, and re-layouts, on_device(): sorted_owner = owner_flat[order]  45.5 us
    mul x16, other arithmetic, kernel_weight(): return 0.25 * (1.0 + jnp.cos(0.5 * math.pi * distance))  20.8 us
  transfers between devices with their start and end apart: 10, of which 5 were waited for; matrix products, arithmetic and copies ran while one was open for 40% of the time, Pallas kernels for 0%

profile of v1, /device:TPU:0, one launch (start us, length us, event | category | flops | bytes accessed | tf_op | source)
XLA Modules:
  0.0 703.4 jit_solution(13962440777952094728)
XLA Ops:
  1.4 4.9 collective-permute-start.1
  7.6 7.5 %sort.17 = (s32[8192]{0:T(1024)}, s32[8192]{0:T(1024)S(1)}) sort(s32[8192]{0:T(1024)} %bitcast.1449, s32[8192]{0:T(1024)S(1)} %iota.38), dimensions={0}, to_apply=%region_0.1 | sort | flops 106496 | bytes 131072 | tf_op jit(solution)/shard_map/jit(argsort)/sort | solution.py:116
  15.2 45.5 %gather_fusion = s32[8192]{0:T(1024)S(1)} fusion(s32[8192]{0:T(1024)S(1)} %bitcast.1450, s32[8192]{0:T(1024)S(1)} %fusion.372), kind=kCustom, calls=%fused_computation | custom fusion | bytes 98304 | tf_op jit(solution)/shard_map/gather | solution.py:117
  62.0 45.5 %gather_fusion.1 = s32[8192]{0:T(1024)S(1)} fusion(s32[8192]{0:T(1024)S(1)} %bitcast.1448, s32[8192]{0:T(1024)S(1)} %fusion.372), kind=kCustom, calls=%fused_computation.2 | custom fusion | bytes 98304 | tf_op jit(solution)/shard_map/gather | solution.py:124
  107.5 31.1 %scatter_custom_fusion.1 = s32[16384]{0:T(1024)} fusion(s32[8192]{0:T(1024)S(1)} %broadcast_select_fusion, s32[8192]{0:T(1024)S(1)} %gather_fusion.1, s32[]{:T(128)} %constant.337.clone.1), kind=kCustom, calls=%fused_computation.697 | custom fusion | bytes 65540
  138.6 7.1 %all-to-all-start.1 = ((s32[1,32,512]{2,0,1:T(1,128)}), s32[1,32,512]{2,0,1:T(1,128)}, u32[]{:S(2)}, u32[]{:S(2)}) async-start(s32[1,32,512]{2,0,1:T(1,128)} %bitcast.41), calls=%async_computation.1 | async-start | bytes 131072 | tf_op jit(solution)/shard_map/all_to_all | solution.py:141
  146.2 3.6 collective-permute-start.3
  151.2 4.1 collective-permute-done.2
  155.6 2.6 copy.287
  158.3 70.9 %scatter_custom_fusion = f32[6,16384]{0,1:T(8,128)} fusion(s32[8192]{0:T(1024)S(1)} %bitcast.1484, f32[6,8192]{0,1:T(8,128)} %copy.287, s32[8192]{0:T(1024)S(1)} %fusion.372, f32[]{:T(128)} %constant.338.clone.1), kind=kCustom, calls=%fused_computation.104 | custom fusion | bytes 393728 | tf_op jit(solution)/shard_map/scatter | solution.py:123
  229.2 3.7 fusion.383
  232.8 3.7 fusion.382
  238.2 1.7 copy.365
  239.9 1.7 copy.366
  243.2 1.7 copy.368
  244.9 1.7 copy.369
  248.2 1.7 copy.371
  251.5 1.7 copy.373
  253.1 1.7 copy.374
  290.6 5.5 all-to-all-start
  297.2 12.4 %all-to-all-done = f32[32,6,1,512]{3,2,1,0:T(1,128)S(1)} async-done(((f32[32,6,1,512]{3,2,1,0:T(1,128)}), f32[32,6,1,512]{3,2,1,0:T(1,128)S(1)}, u32[]{:S(2)}, u32[]{:S(2)}) %all-to-all-start) | async-done | bytes 393248 | tf_op jit(solution)/shard_map/all_to_all | solution.py:127
  309.8 253.6 %while.18 = (s32[]{:T(128)}, f32[3840,256]{1,0:T(8,128)}, f32[16,6,1024]{2,0,1:T(8,128)S(1)}, s32[16,1024]{1,0:T(8,128)S(1)}, s32[]{:T(128)}, /*index=5*/s32[]{:T(128)}, s32[]{}, s32[]{}, s32[]{}) while((s32[]{:T(128)}, f32[3840,256]{1,0:T(8,128)}, f32[16,6,1024]{2,0,1:T(8,128)S(1)}, s32[16,1024]{1,0:T(8,128)S(1)}, ...), condition=%wide.region_7.8_spmd.clone.clone, body=%wide.region_6.7_spmd.clone.clone.sunk | while | flops 2029383680 | bytes 26144940 | solution.py:197
  311.7 5.4 multiply_convert_fusion.2
  317.1 7.5 %convolution_add_fusion.2 = f32[3840,256]{1,0:T(8,128)} fusion(bf16[1024,3840]{0,1:T(8,128)(2,1)} %bitcast.1451, f32[3840,256]{1,0:T(8,128)} %get-tuple-element.470, pred[]{:T(512)S(6)} %compare.117, f32[1024]{0:T(1024)S(1)} %bitcast.1490, s32[1024]{0:T(1024)S(1)} %get-tuple-element.453, f32[1024]{0:T(1024)S(1)} %bitcast.1489, ...), kind=kOutput, calls=%fused_computation.8.clone.1 | convolution fusion | flops 2018377728 | bytes 15761409 | tf_op jit(solution)/shard_map/while/body/eval_jaxpr/dot_general | solution.py:192
  326.5 5.4 multiply_convert_fusion.2
  331.9 8.6 %convolution_add_fusion.2 = f32[3840,256]{1,0:T(8,128)} fusion(bf16[1024,3840]{0,1:T(8,128)(2,1)} %bitcast.1451, f32[3840,256]{1,0:T(8,128)} %get-tuple-element.470, pred[]{:T(512)S(6)} %compare.117, f32[1024]{0:T(1024)S(1)} %bitcast.1490, s32[1024]{0:T(1024)S(1)} %get-tuple-element.453, f32[1024]{0:T(1024)S(1)} %bitcast.1489, ...), kind=kOutput, calls=%fused_computation.8.clone.1 | convolution fusion | flops 2018377728 | bytes 15761409 | tf_op jit(solution)/shard_map/while/body/eval_jaxpr/dot_general | solution.py:192
  342.4 5.4 multiply_convert_fusion.2
  347.8 8.6 %convolution_add_fusion.2 = f32[3840,256]{1,0:T(8,128)} fusion(bf16[1024,3840]{0,1:T(8,128)(2,1)} %bitcast.1451, f32[3840,256]{1,0:T(8,128)} %get-tuple-element.470, pred[]{:T(512)S(6)} %compare.117, f32[1024]{0:T(1024)S(1)} %bitcast.1490, s32[1024]{0:T(1024)S(1)} %get-tuple-element.453, f32[1024]{0:T(1024)S(1)} %bitcast.1489, ...), kind=kOutput, calls=%fused_computation.8.clone.1 | convolution fusion | flops 2018377728 | bytes 15761409 | tf_op jit(solution)/shard_map/while/body/eval_jaxpr/dot_general | solution.py:192
  358.3 5.4 multiply_convert_fusion.2
  363.7 8.6 %convolution_add_fusion.2 = f32[3840,256]{1,0:T(8,128)} fusion(bf16[1024,3840]{0,1:T(8,128)(2,1)} %bitcast.1451, f32[3840,256]{1,0:T(8,128)} %get-tuple-element.470, pred[]{:T(512)S(6)} %compare.117, f32[1024]{0:T(1024)S(1)} %bitcast.1490, s32[1024]{0:T(1024)S(1)} %get-tuple-element.453, f32[1024]{0:T(1024)S(1)} %bitcast.1489, ...), kind=kOutput, calls=%fused_computation.8.clone.1 | convolution fusion | flops 2018377728 | bytes 15761409 | tf_op jit(solution)/shard_map/while/body/eval_jaxpr/dot_general | solution.py:192
  374.2 5.4 multiply_convert_fusion.2
  379.6 8.6 %convolution_add_fusion.2 = f32[3840,256]{1,0:T(8,128)} fusion(bf16[1024,3840]{0,1:T(8,128)(2,1)} %bitcast.1451, f32[3840,256]{1,0:T(8,128)} %get-tuple-element.470, pred[]{:T(512)S(6)} %compare.117, f32[1024]{0:T(1024)S(1)} %bitcast.1490, s32[1024]{0:T(1024)S(1)} %get-tuple-element.453, f32[1024]{0:T(1024)S(1)} %bitcast.1489, ...), kind=kOutput, calls=%fused_computation.8.clone.1 | convolution fusion | flops 2018377728 | bytes 15761409 | tf_op jit(solution)/shard_map/while/body/eval_jaxpr/dot_general | solution.py:192
  390.1 5.4 multiply_convert_fusion.2
  395.5 8.6 %convolution_add_fusion.2 = f32[3840,256]{1,0:T(8,128)} fusion(bf16[1024,3840]{0,1:T(8,128)(2,1)} %bitcast.1451, f32[3840,256]{1,0:T(8,128)} %get-tuple-element.470, pred[]{:T(512)S(6)} %compare.117, f32[1024]{0:T(1024)S(1)} %bitcast.1490, s32[1024]{0:T(1024)S(1)} %get-tuple-element.453, f32[1024]{0:T(1024)S(1)} %bitcast.1489, ...), kind=kOutput, calls=%fused_computation.8.clone.1 | convolution fusion | flops 2018377728 | bytes 15761409 | tf_op jit(solution)/shard_map/while/body/eval_jaxpr/dot_general | solution.py:192
  406.0 5.4 multiply_convert_fusion.2
  411.4 8.6 %convolution_add_fusion.2 = f32[3840,256]{1,0:T(8,128)} fusion(bf16[1024,3840]{0,1:T(8,128)(2,1)} %bitcast.1451, f32[3840,256]{1,0:T(8,128)} %get-tuple-element.470, pred[]{:T(512)S(6)} %compare.117, f32[1024]{0:T(1024)S(1)} %bitcast.1490, s32[1024]{0:T(1024)S(1)} %get-tuple-element.453, f32[1024]{0:T(1024)S(1)} %bitcast.1489, ...), kind=kOutput, calls=%fused_computation.8.clone.1 | convolution fusion | flops 2018377728 | bytes 15761409 | tf_op jit(solution)/shard_map/while/body/eval_jaxpr/dot_general | solution.py:192
  422.0 5.4 multiply_convert_fusion.2
  427.4 8.6 %convolution_add_fusion.2 = f32[3840,256]{1,0:T(8,128)} fusion(bf16[1024,3840]{0,1:T(8,128)(2,1)} %bitcast.1451, f32[3840,256]{1,0:T(8,128)} %get-tuple-element.470, pred[]{:T(512)S(6)} %compare.117, f32[1024]{0:T(1024)S(1)} %bitcast.1490, s32[1024]{0:T(1024)S(1)} %get-tuple-element.453, f32[1024]{0:T(1024)S(1)} %bitcast.1489, ...), kind=kOutput, calls=%fused_computation.8.clone.1 | convolution fusion | flops 2018377728 | bytes 15761409 | tf_op jit(solution)/shard_map/while/body/eval_jaxpr/dot_general | solution.py:192
  437.9 5.4 multiply_convert_fusion.2
  443.3 8.6 %convolution_add_fusion.2 = f32[3840,256]{1,0:T(8,128)} fusion(bf16[1024,3840]{0,1:T(8,128)(2,1)} %bitcast.1451, f32[3840,256]{1,0:T(8,128)} %get-tuple-element.470, pred[]{:T(512)S(6)} %compare.117, f32[1024]{0:T(1024)S(1)} %bitcast.1490, s32[1024]{0:T(1024)S(1)} %get-tuple-element.453, f32[1024]{0:T(1024)S(1)} %bitcast.1489, ...), kind=kOutput, calls=%fused_computation.8.clone.1 | convolution fusion | flops 2018377728 | bytes 15761409 | tf_op jit(solution)/shard_map/while/body/eval_jaxpr/dot_general | solution.py:192
  453.8 5.4 multiply_convert_fusion.2
  459.2 8.6 %convolution_add_fusion.2 = f32[3840,256]{1,0:T(8,128)} fusion(bf16[1024,3840]{0,1:T(8,128)(2,1)} %bitcast.1451, f32[3840,256]{1,0:T(8,128)} %get-tuple-element.470, pred[]{:T(512)S(6)} %compare.117, f32[1024]{0:T(1024)S(1)} %bitcast.1490, s32[1024]{0:T(1024)S(1)} %get-tuple-element.453, f32[1024]{0:T(1024)S(1)} %bitcast.1489, ...), kind=kOutput, calls=%fused_computation.8.clone.1 | convolution fusion | flops 2018377728 | bytes 15761409 | tf_op jit(solution)/shard_map/while/body/eval_jaxpr/dot_general | solution.py:192
  469.7 5.4 multiply_convert_fusion.2
  475.1 8.6 %convolution_add_fusion.2 = f32[3840,256]{1,0:T(8,128)} fusion(bf16[1024,3840]{0,1:T(8,128)(2,1)} %bitcast.1451, f32[3840,256]{1,0:T(8,128)} %get-tuple-element.470, pred[]{:T(512)S(6)} %compare.117, f32[1024]{0:T(1024)S(1)} %bitcast.1490, s32[1024]{0:T(1024)S(1)} %get-tuple-element.453, f32[1024]{0:T(1024)S(1)} %bitcast.1489, ...), kind=kOutput, calls=%fused_computation.8.clone.1 | convolution fusion | flops 2018377728 | bytes 15761409 | tf_op jit(solution)/shard_map/while/body/eval_jaxpr/dot_general | solution.py:192
  485.6 5.4 multiply_convert_fusion.2
  491.0 8.6 %convolution_add_fusion.2 = f32[3840,256]{1,0:T(8,128)} fusion(bf16[1024,3840]{0,1:T(8,128)(2,1)} %bitcast.1451, f32[3840,256]{1,0:T(8,128)} %get-tuple-element.470, pred[]{:T(512)S(6)} %compare.117, f32[1024]{0:T(1024)S(1)} %bitcast.1490, s32[1024]{0:T(1024)S(1)} %get-tuple-element.453, f32[1024]{0:T(1024)S(1)} %bitcast.1489, ...), kind=kOutput, calls=%fused_computation.8.clone.1 | convolution fusion | flops 2018377728 | bytes 15761409 | tf_op jit(solution)/shard_map/while/body/eval_jaxpr/dot_general | solution.py:192
  501.5 5.4 multiply_convert_fusion.2
  506.9 8.6 %convolution_add_fusion.2 = f32[3840,256]{1,0:T(8,128)} fusion(bf16[1024,3840]{0,1:T(8,128)(2,1)} %bitcast.1451, f32[3840,256]{1,0:T(8,128)} %get-tuple-element.470, pred[]{:T(512)S(6)} %compare.117, f32[1024]{0:T(1024)S(1)} %bitcast.1490, s32[1024]{0:T(1024)S(1)} %get-tuple-element.453, f32[1024]{0:T(1024)S(1)} %bitcast.1489, ...), kind=kOutput, calls=%fused_computation.8.clone.1 | convolution fusion | flops 2018377728 | bytes 15761409 | tf_op jit(solution)/shard_map/while/body/eval_jaxpr/dot_general | solution.py:192
  517.4 5.4 multiply_convert_fusion.2
  522.8 8.6 %convolution_add_fusion.2 = f32[3840,256]{1,0:T(8,128)} fusion(bf16[1024,3840]{0,1:T(8,128)(2,1)} %bitcast.1451, f32[3840,256]{1,0:T(8,128)} %get-tuple-element.470, pred[]{:T(512)S(6)} %compare.117, f32[1024]{0:T(1024)S(1)} %bitcast.1490, s32[1024]{0:T(1024)S(1)} %get-tuple-element.453, f32[1024]{0:T(1024)S(1)} %bitcast.1489, ...), kind=kOutput, calls=%fused_computation.8.clone.1 | convolution fusion | flops 2018377728 | bytes 15761409 | tf_op jit(solution)/shard_map/while/body/eval_jaxpr/dot_general | solution.py:192
  533.4 5.4 multiply_convert_fusion.2
  538.8 8.6 %convolution_add_fusion.2 = f32[3840,256]{1,0:T(8,128)} fusion(bf16[1024,3840]{0,1:T(8,128)(2,1)} %bitcast.1451, f32[3840,256]{1,0:T(8,128)} %get-tuple-element.470, pred[]{:T(512)S(6)} %compare.117, f32[1024]{0:T(1024)S(1)} %bitcast.1490, s32[1024]{0:T(1024)S(1)} %get-tuple-element.453, f32[1024]{0:T(1024)S(1)} %bitcast.1489, ...), kind=kOutput, calls=%fused_computation.8.clone.1 | convolution fusion | flops 2018377728 | bytes 15761409 | tf_op jit(solution)/shard_map/while/body/eval_jaxpr/dot_general | solution.py:192
  549.3 5.4 multiply_convert_fusion.2
  554.7 8.6 %convolution_add_fusion.2 = f32[3840,256]{1,0:T(8,128)} fusion(bf16[1024,3840]{0,1:T(8,128)(2,1)} %bitcast.1451, f32[3840,256]{1,0:T(8,128)} %get-tuple-element.470, pred[]{:T(512)S(6)} %compare.117, f32[1024]{0:T(1024)S(1)} %bitcast.1490, s32[1024]{0:T(1024)S(1)} %get-tuple-element.453, f32[1024]{0:T(1024)S(1)} %bitcast.1489, ...), kind=kOutput, calls=%fused_computation.8.clone.1 | convolution fusion | flops 2018377728 | bytes 15761409 | tf_op jit(solution)/shard_map/while/body/eval_jaxpr/dot_general | solution.py:192
  563.3 3.7 fusion.384
  569.2 4.6 collective-permute-start.5
  573.8 4.7 reduce_sum.34
  578.5 40.7 %collective-permute-done.4 = f32[2,3,256,256]{3,2,1,0:T(8,128)} collective-permute-done((f32[2,3,256,256]{3,2,1,0:T(8,128)}, f32[2,3,256,256]{3,2,1,0:T(8,128)}, u32[]{:S(2)}, u32[]{:S(2)}) %collective-permute-start.4) | collective-permute-done | bytes 1572896 | tf_op jit(solution)/shard_map/ppermute | solution.py:50
  619.1 2.2 add.2902
  623.9 5.9 fusion.77
  629.9 2.4 fusion.174
  639.9 1.7 fusion.160
  645.1 50.1 %collective-permute-done.6 = f32[5,256,256]{2,1,0:T(8,128)S(1)} collective-permute-done((f32[5,256,256]{2,1,0:T(8,128)S(1)}, f32[5,256,256]{2,1,0:T(8,128)S(1)}, u32[]{:S(2)}, u32[]{:S(2)}) %collective-permute-start.6) | collective-permute-done | bytes 1310752 | tf_op jit(solution)/shard_map/ppermute | solution.py:50
  699.2 3.9 copy-done.7
  (329 shorter events, 97.4 us)
Async XLA Ops:
  0.6 61.3 %copy-start = (s32[2,32,128]{2,1,0:T(8,128)S(1)}, s32[2,32,128]{2,1,0:T(8,128)}, u32[]{:S(2)}) copy-start(s32[2,32,128]{2,1,0:T(8,128)} %param.20) | copy-start | bytes 98308
  0.6 14.5 %copy-start.2 = (s32[2,32,128]{2,1,0:T(8,128)S(1)}, s32[2,32,128]{2,1,0:T(8,128)}, u32[]{:S(2)}) copy-start(s32[2,32,128]{2,1,0:T(8,128)} %param.19) | copy-start | bytes 98308
  1.4 144.5 %collective-permute-start.1 = (f32[3,2,1,128]{3,2,1,0:T(1,128)S(1)}, f32[3,2,1,128]{3,2,1,0:T(1,128)S(1)}, u32[]{:S(2)}, u32[]{:S(2)}) collective-permute-start(f32[3,2,1,128]{3,2,1,0:T(1,128)S(1)} %get-tuple-element.382), channel_id=1, source_target_pairs={{0,1},{1,2},{2,3},{3,4},{4,5},{5,6},{6,7},{8,9},{9,10},{10,11},{11... | collective-permute-start | bytes 9224 | tf_op jit(solution)/shard_map/ppermute | solution.py:41
  6.3 139.6 %collective-permute-start = (f32[3,2,1,128]{3,2,1,0:T(1,128)S(1)}, f32[3,2,1,128]{3,2,1,0:T(1,128)S(1)}, u32[]{:S(2)}, u32[]{:S(2)}) collective-permute-start(f32[3,2,1,128]{3,2,1,0:T(1,128)S(1)} %get-tuple-element.381), channel_id=1, source_target_pairs={{1,0},{2,1},{3,2},{4,3},{5,4},{6,5},{7,6},{9,8},{10,9},{11,10},{12... | collective-permute-start | bytes 9224 | tf_op jit(solution)/shard_map/ppermute | solution.py:42
  15.2 46.4 %copy-start.11 = (s32[2]{0:T(128)S(1)}, s32[2]{0:T(128)}, u32[]{:S(2)}) copy-start(s32[2]{0:T(128)} %constant.369) | copy-start | bytes 28
  15.2 46.6 %copy-start.10 = (s32[2]{0:T(128)S(1)}, s32[2]{0:T(128)}, u32[]{:S(2)}) copy-start(s32[2]{0:T(128)} %constant.366) | copy-start | bytes 28
  61.9 83.8 %copy-start.4 = (f32[3,2,32,128]{3,2,1,0:T(8,128)S(1)}, f32[3,2,32,128]{3,2,1,0:T(8,128)}, u32[]{:S(2)}) copy-start(f32[3,2,32,128]{3,2,1,0:T(8,128)} %param.15) | copy-start | bytes 294916
  62.0 93.3 %copy-start.8 = (f32[2]{0:T(128)S(1)}, f32[2]{0:T(128)}, u32[]{:S(2)}) copy-start(f32[2]{0:T(128)} %param.17) | copy-start | bytes 28
  62.0 93.3 %copy-start.9 = (f32[2]{0:T(128)S(1)}, f32[2]{0:T(128)}, u32[]{:S(2)}) copy-start(f32[2]{0:T(128)} %param.16) | copy-start | bytes 28
  62.0 93.4 %copy-start.6 = (f32[3,2,32,128]{3,2,1,0:T(8,128)S(1)}, f32[3,2,32,128]{3,2,1,0:T(8,128)}, u32[]{:S(2)}) copy-start(f32[3,2,32,128]{3,2,1,0:T(8,128)} %param.18) | copy-start | bytes 294916
  138.6 152.0 %all-to-all-start.1 = ((s32[1,32,512]{2,0,1:T(1,128)}), s32[1,32,512]{2,0,1:T(1,128)}, u32[]{:S(2)}, u32[]{:S(2)}) async-start(s32[1,32,512]{2,0,1:T(1,128)} %bitcast.41), calls=%async_computation.1 | async-start | bytes 131072 | tf_op jit(solution)/shard_map/all_to_all | solution.py:141
  146.2 5.0 collective-permute-start.3
  149.8 5.5 collective-permute-start.2
  155.4 73.7 %copy-start.5 = (f32[3,2,32,128]{3,2,1,0:T(8,128)}, f32[3,2,32,128]{3,2,1,0:T(8,128)S(1)}, u32[]{:S(2)}) copy-start(f32[3,2,32,128]{3,2,1,0:T(8,128)S(1)} %fusion.366) | copy-start | bytes 294916
  290.6 18.9 %all-to-all-start = ((f32[32,6,1,512]{3,2,1,0:T(1,128)}), f32[32,6,1,512]{3,2,1,0:T(1,128)S(1)}, u32[]{:S(2)}, u32[]{:S(2)}) async-start(f32[32,6,1,512]{3,2,1,0:T(1,128)} %constant_dynamic-update-slice_fusion), calls=%async_computation | async-start | bytes 786432 | tf_op jit(solution)/shard_map/all_to_all | solution.py:127
  567.1 52.1 %collective-permute-start.4 = (f32[2,3,256,256]{3,2,1,0:T(8,128)}, f32[2,3,256,256]{3,2,1,0:T(8,128)}, u32[]{:S(2)}, u32[]{:S(2)}) collective-permute-start(f32[2,3,256,256]{3,2,1,0:T(8,128)} %bitcast.43), channel_id=1, source_target_pairs={{0,1},{1,2},{2,3},{3,4},{4,5},{5,6},{6,7},{7,8},{8,9},{9,10},{10,1... | collective-permute-start | bytes 4718600 | tf_op jit(solution)/shard_map/ppermute | solution.py:50
  569.2 53.3 %collective-permute-start.5 = (f32[1,3,256,256]{3,2,1,0:T(8,128)S(1)}, f32[1,3,256,256]{3,2,1,0:T(8,128)}, u32[]{:S(2)}, u32[]{:S(2)}) collective-permute-start(f32[1,3,256,256]{3,2,1,0:T(8,128)S(1)} %bitcast.1472), channel_id=1, source_target_pairs={{0,31},{1,0},{2,1},{3,2},{4,3},{5,4},{6,5},{7,6},{8,7},{9,8},{10,9... | collective-permute-start | bytes 2359304 | tf_op jit(solution)/shard_map/ppermute | solution.py:50
  573.8 56.0 %slice-start = ((s8[9961472]{0:T(1024)(128)(4,1)}), s8[1572864]{0:T(1024)(128)(4,1)S(1)}, s32[]{:S(2)}) async-start(s8[9961472]{0:T(1024)(128)(4,1)} %bitcast.1452), calls=%async_computation.2 | async-start | bytes 3145728
  619.1 10.7 %slice-start.1 = ((s8[9961472]{0:T(1024)(128)(4,1)}), s8[4194304]{0:T(1024)(128)(4,1)S(1)}, s32[]{:S(2)}) async-start(s8[9961472]{0:T(1024)(128)(4,1)} %bitcast.1452), calls=%async_computation.3 | async-start | bytes 8388608
  623.9 73.5 %copy-start.3 = (f32[2,3,256,256]{3,2,1,0:T(8,128)}, f32[2,3,256,256]{3,2,1,0:T(8,128)S(1)}, u32[]{:S(2)}) copy-start(f32[2,3,256,256]{3,2,1,0:T(8,128)S(1)} %fusion.29) | copy-start | bytes 4718596
  623.9 6.0 slice-start.2
  637.3 59.0 %collective-permute-start.7 = (f32[5,256,256]{2,1,0:T(8,128)S(1)}, f32[5,256,256]{2,1,0:T(8,128)S(1)}, u32[]{:S(2)}, u32[]{:S(2)}) collective-permute-start(f32[5,256,256]{2,1,0:T(8,128)S(1)} %get-tuple-element.363), channel_id=1, source_target_pairs={{0,31},{1,0},{2,1},{3,2},{4,3},{5,4},{6,5},{7,6},{8,7},{9,8},{10,9... | collective-permute-start | bytes 3932168 | tf_op jit(solution)/shard_map/ppermute | solution.py:50
  638.4 56.8 %collective-permute-start.6 = (f32[5,256,256]{2,1,0:T(8,128)S(1)}, f32[5,256,256]{2,1,0:T(8,128)S(1)}, u32[]{:S(2)}, u32[]{:S(2)}) collective-permute-start(f32[5,256,256]{2,1,0:T(8,128)S(1)} %get-tuple-element.370), channel_id=1, source_target_pairs={{0,1},{1,2},{2,3},{3,4},{4,5},{5,6},{6,7},{7,8},{8,9},{9,10},{10,1... | collective-permute-start | bytes 3932168 | tf_op jit(solution)/shard_map/ppermute | solution.py:50
  698.1 5.0 copy-start.1
  699.2 3.9 copy-start.7
